TPU v7x, 512 devices: a whole 4x4x16 slice. The times are simulated.
512 devices in a mesh: pair: 64 (over z, x), virt: 8 (over y, core).
Axes of the slice: x: 4, y: 4, z: 16, core: 2. Of those that a mesh axis runs over, the one named last changes fastest.
Arguments:
- amplitudes: bfloat16 [256, 1024, 1024], P('pair', None, 'virt'), may hold values from -0.1796875 to 0.1796875
- cholesky: bfloat16 [8, 1024, 1792], P(None, 'virt', 'pair'), may hold values from -0.1640625 to 0.1640625
- energy_first: float32 [32], replicated, may hold values from -3 to -0.3
- energy_second: float32 [8], replicated, may hold values from -3 to -0.3
- energy_virtual: float32 [1024], replicated, may hold values from 0.2 to 4
Outputs:
- residual: bfloat16 [256, 1024, 1024], P('pair', None, 'virt')
All inputs are finite; a program needn't handle non-finite values.
Results may differ from a plain program's by a relative error of at most 0.0095.
Values may be sent and summed in bfloat16 or wider, within the bound.
A program may use at most 64 MiB of HBM per device.

v0:
```python
import jax
import jax.numpy as jnp
from jax import lax
from jax.sharding import Mesh
from jax.sharding import PartitionSpec as P

OCC = 8
PAIR = ("pair_0", "pair_1")


def joined_along(pieces, dim):
    dims = list(pieces.shape[1:])
    dims[dim] *= pieces.shape[0]
    return jnp.moveaxis(pieces, 0, dim).reshape(dims)


def stacked_from(x, axes, sequence):
    pieces = x[None]
    for k in sequence:
        pieces = lax.all_gather(pieces, axes[k], axis=0, tiled=True)
    held = [lax.axis_size(axes[k]) for k in reversed(sequence)]
    pieces = pieces.reshape(*held, *x.shape)
    turned = sorted(range(len(sequence)), key=lambda place: sequence[len(sequence) - 1 - place])
    return pieces.transpose(*turned, *range(len(sequence), pieces.ndim)).reshape(-1, *x.shape)


def gather_axes(x, axes, sequence, dim):
    return joined_along(stacked_from(x, axes, sequence), dim)


def in_blocks(x, dim, devices):
    dims = x.shape
    pieces = x.reshape(*dims[:dim], devices, dims[dim] // devices, *dims[dim + 1 :])
    return jnp.moveaxis(pieces, dim, 0)


def sum_at_owner(x, axis, dim):
    pieces = in_blocks(x, dim, lax.axis_size(axis))
    arrived = lax.all_to_all(pieces, axis, split_axis=0, concat_axis=0, tiled=True)
    return arrived.astype(jnp.float32).sum(axis=0)


def from_partner(x, axis, bit):
    return lax.ppermute(x, axis, [(i, i ^ 1 << bit) for i in range(lax.axis_size(axis))])


def from_everyone(x, axis):
    devices = lax.axis_size(axis)
    return lax.all_to_all(jnp.broadcast_to(x[None], (devices, *x.shape)), axis, 0, 0, tiled=True)


def collect(x, axis, dim):
    return joined_along(from_everyone(x, axis), dim)


def on_device(amplitudes, cholesky, energy_first, energy_second, energy_virtual):
    pair_count, virtual_count, local_virtual = amplitudes.shape
    tiles_count = lax.axis_size("virt")
    first_count = max(pair_count // OCC, 1)
    second_count = pair_count // first_count
    offset = lax.axis_index(PAIR) * pair_count
    first_start = offset // OCC
    second_start = offset % OCC
    column_start = lax.axis_index("virt") * local_virtual
    blocks = amplitudes.reshape(pair_count, tiles_count, local_virtual, local_virtual)
    arrived = lax.all_to_all(blocks, "virt", split_axis=1, concat_axis=1, tiled=True)
    mirrored = jnp.swapaxes(arrived, 2, 3).reshape(pair_count, virtual_count, local_virtual)
    combined = (2.0 * amplitudes.astype(jnp.float32) - mirrored.astype(jnp.float32)).astype(
        jnp.bfloat16
    )
    combined = combined.reshape(first_count, second_count, virtual_count, local_virtual)
    vectors = gather_axes(cholesky, PAIR, (0, 1), 2)
    chosen = lax.dynamic_slice_in_dim(vectors, second_start, second_count, 0)
    half_width = chosen.shape[2] // 2
    pieces = []
    for part_index in range(2):
        picked = chosen[:, :, part_index * half_width : (part_index + 1) * half_width]
        partial_value = jnp.einsum(
            "ilad,ldq->iaq", combined, picked, preferred_element_type=jnp.float32
        )
        tile_sum = sum_at_owner(partial_value.astype(jnp.bfloat16), "virt", 2).astype(jnp.bfloat16)
        collected = tile_sum[None]
        collected = jnp.concatenate([collected, from_partner(collected, PAIR, 0)], axis=0)
        summed = jnp.sum(collected.astype(jnp.float32), axis=0).astype(jnp.bfloat16)
        pieces.append(collect(summed, "virt", 2))
    reduced = jnp.concatenate(pieces, axis=2)
    cycle_term = jnp.einsum("iaq,lbq->ilab", reduced, chosen, preferred_element_type=jnp.float32)
    first_energy = lax.dynamic_slice_in_dim(energy_first, first_start, first_count, 0)
    second_energy = lax.dynamic_slice_in_dim(energy_second, second_start, second_count, 0)
    column_energy = lax.dynamic_slice_in_dim(energy_virtual, column_start, local_virtual, 0)
    virtual_pairs = energy_virtual[:, None] + column_energy[None, :]
    diagonal = (
        virtual_pairs[None, None, :, :]
        - first_energy[:, None, None, None]
        - second_energy[None, :, None, None]
    )
    values = amplitudes.reshape(first_count, second_count, virtual_count, local_virtual).astype(
        jnp.float32
    )
    result = diagonal * values + cycle_term
    return result.reshape(pair_count, virtual_count, local_virtual).astype(jnp.bfloat16)


def solution(mesh):
    finer = Mesh(mesh.devices.reshape(16, 4, mesh.shape["virt"]), ("pair_0", "pair_1", "virt"))
    placed = (P(PAIR, None, "virt"), P(None, "virt", PAIR), P(), P(), P())
    return jax.shard_map(
        on_device, mesh=finer, in_specs=placed, out_specs=P(PAIR, None, "virt"), check_vma=False
    )
```

profile of v0, /device:TPU:1, one launch (start us, length us, event | category | flops | bytes accessed | tf_op | source)
XLA Modules:
  0.0 244.4 jit_solution(900397988528730859)
XLA Ops:
  6.5 37.6 %all-gather = bf16[128,128,28]{1,0,2:T(8,128)(2,1)} all-gather(bf16[8,128,28]{1,0,2:T(8,128)(2,1)} %param.6), channel_id=2, replica_groups=mesh['pair_0'=16,'pair_1'=4,'virt'=8] {'pair_0'}, dimensions={0}, use_global_device_ids=true | all-gather | bytes 974848 | tf_op jit(solution)/shard_map/all_gather | solution.py:20
  44.1 1.0 copy.61
  45.2 11.7 %all-to-all-start = ((bf16[4,8,128,128]{3,2,0,1:T(8,128)(2,1)}), bf16[4,8,128,128]{3,2,0,1:T(8,128)(2,1)}, u32[]{:S(2)}, u32[]{:S(2)}) async-start(bf16[4,8,128,128]{3,2,0,1:T(8,128)(2,1)} %copy.61), calls=%async_computation | async-start | bytes 2097152 | tf_op jit(solution)/shard_map/all_to_all | solution.py:66
  57.5 41.0 %all-gather.3.cloned.1.call-done = bf16[64,8,128,28]{2,1,0,3:T(8,128)(2,1)} async-done(((bf16[16,8,128,28]{2,1,0,3:T(8,128)(2,1)}), bf16[64,8,128,28]{2,1,0,3:T(8,128)(2,1)}) %all-gather.3.cloned.1.call-update) | async-done | bytes 3670032 | tf_op jit(solution)/shard_map/all_gather | solution.py:20
  98.5 3.0 %copy.59 = bf16[16,4,8,128,28]{3,2,4,1,0:T(8,128)(2,1)S(1)} copy(bf16[16,4,8,128,28]{3,2,0,1,4:T(8,128)(2,1)} %bitcast.79) | data formatting | bytes 7340032 | tf_op jit(solution)/shard_map/transpose | solution.py:24
  101.4 1.0 constant_dynamic-slice_fusion
  102.5 1.2 copy-done.2
  104.0 4.3 %bitcast_convert_fusion.1 = bf16[1024,896]{0,1:T(8,128)(2,1)} fusion(bf16[4,128,1792]{1,2,0:T(8,128)(2,1)S(1)} %copy.77, bf16[4,1024,128]{1,2,0:T(8,128)(2,1)S(1)} %copy.57, bf16[4,8,128,128]{3,2,0,1:T(8,128)(2,1)} %all-to-all-done), kind=kOutput, calls=%fused_computation.5 | convolution fusion | flops 943063040 | bytes 4849664 | tf_op jit(solution)/shard_map/ilad,ldq->iaq/dot_general | solution.py:78
  108.3 5.1 %all-to-all-start.1 = ((bf16[8,1,1024,112]{2,3,1,0:T(8,128)(2,1)}), bf16[8,1,1024,112]{2,3,1,0:T(8,128)(2,1)S(1)}, u32[]{:S(2)}, u32[]{:S(2)}) async-start(bf16[8,1,1024,112]{2,3,1,0:T(8,128)(2,1)} %bitcast.82), calls=%async_computation.1 | async-start | bytes 3670016 | tf_op jit(solution)/shard_map/all_to_all | solution.py:39
  113.4 3.9 %bitcast_convert_fusion = bf16[1024,896]{0,1:T(8,128)(2,1)} fusion(bf16[4,128,1792]{1,2,0:T(8,128)(2,1)} %copy-done.5, bf16[4,1024,128]{1,2,0:T(8,128)(2,1)S(1)} %copy.57, bf16[4,8,128,128]{3,2,0,1:T(8,128)(2,1)} %all-to-all-done), kind=kOutput, calls=%fused_computation.4 | convolution fusion | flops 943063040 | bytes 4849664 | tf_op jit(solution)/shard_map/ilad,ldq->iaq/dot_general | solution.py:78
  117.3 19.5 %all-to-all-done.1 = bf16[8,1,1024,112]{2,3,1,0:T(8,128)(2,1)S(1)} async-done(((bf16[8,1,1024,112]{2,3,1,0:T(8,128)(2,1)}), bf16[8,1,1024,112]{2,3,1,0:T(8,128)(2,1)S(1)}, u32[]{:S(2)}, u32[]{:S(2)}) %all-to-all-start.1) | async-done | bytes 1835040 | tf_op jit(solution)/shard_map/all_to_all | solution.py:39
  136.8 1.3 copy-done.1
  138.1 4.5 %all-to-all-start.3 = ((bf16[8,1,1024,112]{2,3,1,0:T(8,128)(2,1)}), bf16[8,1,1024,112]{2,3,1,0:T(8,128)(2,1)S(1)}, u32[]{:S(2)}, u32[]{:S(2)}) async-start(bf16[8,1,1024,112]{2,3,1,0:T(8,128)(2,1)} %bitcast.81), calls=%async_computation.3 | async-start | bytes 3670016 | tf_op jit(solution)/shard_map/all_to_all | solution.py:39
  142.6 1.8 reduce_sum.48
  144.4 2.4 collective-permute-start
  146.8 6.5 %collective-permute-done = bf16[1,1,1024,112]{2,3,1,0:T(8,128)(2,1)S(1)} collective-permute-done((bf16[1,1,1024,112]{2,3,1,0:T(8,128)(2,1)S(1)}, bf16[1,1,1024,112]{2,3,1,0:T(8,128)(2,1)S(1)}, u32[]{:S(2)}, u32[]{:S(2)}) %collective-permute-start) | collective-permute-done | bytes 229408 | tf_op jit(solution)/shard_map/ppermute | solution.py:44
  153.4 12.6 %all-to-all-done.3 = bf16[8,1,1024,112]{2,3,1,0:T(8,128)(2,1)S(1)} async-done(((bf16[8,1,1024,112]{2,3,1,0:T(8,128)(2,1)}), bf16[8,1,1024,112]{2,3,1,0:T(8,128)(2,1)S(1)}, u32[]{:S(2)}, u32[]{:S(2)}) %all-to-all-start.3) | async-done | bytes 1835040 | tf_op jit(solution)/shard_map/all_to_all | solution.py:39
  166.0 1.7 broadcast_in_dim.12
  167.9 4.5 %all-to-all-start.2 = ((bf16[8,1,1024,112]{2,3,1,0:T(8,128)(2,1)}), bf16[8,1,1024,112]{2,3,1,0:T(8,128)(2,1)S(1)}, u32[]{:S(2)}, u32[]{:S(2)}) async-start(bf16[8,1,1024,112]{2,3,1,0:T(8,128)(2,1)} %broadcast_in_dim.12), calls=%async_computation.2 | async-start | bytes 3670016 | tf_op jit(solution)/shard_map/all_to_all | solution.py:49
  172.3 1.8 reduce_sum.51
  174.2 2.4 collective-permute-start.1
  176.6 6.5 %collective-permute-done.1 = bf16[1,1,1024,112]{2,3,1,0:T(8,128)(2,1)S(1)} collective-permute-done((bf16[1,1,1024,112]{2,3,1,0:T(8,128)(2,1)S(1)}, bf16[1,1,1024,112]{2,3,1,0:T(8,128)(2,1)S(1)}, u32[]{:S(2)}, u32[]{:S(2)}) %collective-permute-start.1) | collective-permute-done | bytes 229408 | tf_op jit(solution)/shard_map/ppermute | solution.py:44
  183.1 12.6 %all-to-all-done.2 = bf16[8,1,1024,112]{2,3,1,0:T(8,128)(2,1)S(1)} async-done(((bf16[8,1,1024,112]{2,3,1,0:T(8,128)(2,1)}), bf16[8,1,1024,112]{2,3,1,0:T(8,128)(2,1)S(1)}, u32[]{:S(2)}, u32[]{:S(2)}) %all-to-all-start.2) | async-done | bytes 1835040 | tf_op jit(solution)/shard_map/all_to_all | solution.py:49
  195.7 1.5 broadcast_in_dim.14
  197.2 5.3 %all-to-all-start.4 = ((bf16[8,1,1024,112]{2,3,1,0:T(8,128)(2,1)}), bf16[8,1,1024,112]{2,3,1,0:T(8,128)(2,1)}, u32[]{:S(2)}, u32[]{:S(2)}) async-start(bf16[8,1,1024,112]{2,3,1,0:T(8,128)(2,1)} %broadcast_in_dim.14), calls=%async_computation.4 | async-start | bytes 3670016 | tf_op jit(solution)/shard_map/all_to_all | solution.py:49
  202.6 0.6 dynamic_slice.13
  203.3 0.8 add_subtract_fusion
  204.1 2.5 %copy.69 = bf16[1,1024,896]{2,1,0:T(8,128)(2,1)} copy(bf16[1,1024,896]{1,2,0:T(8,128)(2,1)S(1)} %bitcast.77) | data formatting | bytes 3670016 | tf_op jit(solution)/shard_map/reshape | solution.py:14
  206.6 19.5 %all-to-all-done.4 = bf16[8,1,1024,112]{2,3,1,0:T(8,128)(2,1)} async-done(((bf16[8,1,1024,112]{2,3,1,0:T(8,128)(2,1)}), bf16[8,1,1024,112]{2,3,1,0:T(8,128)(2,1)}, u32[]{:S(2)}, u32[]{:S(2)}) %all-to-all-start.4) | async-done | bytes 1835040 | tf_op jit(solution)/shard_map/all_to_all | solution.py:49
  226.1 3.8 %copy.70 = bf16[1,1024,896]{2,1,0:T(8,128)(2,1)} copy(bf16[1,1024,896]{1,2,0:T(8,128)(2,1)} %bitcast.28) | data formatting | bytes 3670016 | tf_op jit(solution)/shard_map/reshape | solution.py:14
  229.9 5.3 %fusion.8 = bf16[4,1024,128]{1,2,0:T(8,128)(2,1)} fusion(bf16[1,1024,896]{2,1,0:T(8,128)(2,1)} %copy.70, bf16[1,1024,896]{2,1,0:T(8,128)(2,1)} %copy.69, bf16[4,1024,128]{1,2,0:T(8,128)(2,1)S(1)} %copy.57, f32[4]{0:T(128)S(1)} %dynamic_slice.14, f32[1024,128]{0,1:T(8,128)S(1)} %add_subtract_fusion, bf16[4,128,1792]{1,0,2:T(4,128)(2,1)S(1)} %copy-done.3), kind=kOutput, calls=%fused_computation.14 | convolution fusion | flops 1889009664 | bytes 8126480 | tf_op jit(solution)/shard_map/iaq,lbq->ilab/dot_general | solution.py:87
  235.3 2.3 copy.72
  (25 shorter events, 1.2 us)
Async XLA Ops:
  6.5 37.6 %copy-start.4 = (bf16[4,1024,128]{2,1,0:T(8,128)(2,1)S(1)}, bf16[4,1024,128]{2,1,0:T(8,128)(2,1)}, u32[]{:S(2)}) copy-start(bf16[4,1024,128]{2,1,0:T(8,128)(2,1)} %param.5) | copy-start | bytes 3145732
  6.5 91.9 %all-gather.3.cloned.1.call-start = ((), (), s32[]{:S(2)}) async-start(), calls=%async_computation.5 | async-start | bytes 4587520 | tf_op jit(solution)/shard_map/all_gather | solution.py:20
  45.2 58.8 %all-to-all-start = ((bf16[4,8,128,128]{3,2,0,1:T(8,128)(2,1)}), bf16[4,8,128,128]{3,2,0,1:T(8,128)(2,1)}, u32[]{:S(2)}, u32[]{:S(2)}) async-start(bf16[4,8,128,128]{3,2,0,1:T(8,128)(2,1)} %copy.61), calls=%async_computation | async-start | bytes 2097152 | tf_op jit(solution)/shard_map/all_to_all | solution.py:66
  102.5 1.3 copy-start.2
  104.0 4.3 %copy-start.5 = (bf16[4,128,1792]{1,2,0:T(8,128)(2,1)}, bf16[4,128,1792]{1,2,0:T(8,128)(2,1)S(1)}, u32[]{:S(2)}) copy-start(bf16[4,128,1792]{1,2,0:T(8,128)(2,1)S(1)} %copy.77) | copy-start | bytes 5505028
  108.3 28.5 %all-to-all-start.1 = ((bf16[8,1,1024,112]{2,3,1,0:T(8,128)(2,1)}), bf16[8,1,1024,112]{2,3,1,0:T(8,128)(2,1)S(1)}, u32[]{:S(2)}, u32[]{:S(2)}) async-start(bf16[8,1,1024,112]{2,3,1,0:T(8,128)(2,1)} %bitcast.82), calls=%async_computation.1 | async-start | bytes 3670016 | tf_op jit(solution)/shard_map/all_to_all | solution.py:39
  136.8 1.3 copy-start.1
  138.1 27.9 %all-to-all-start.3 = ((bf16[8,1,1024,112]{2,3,1,0:T(8,128)(2,1)}), bf16[8,1,1024,112]{2,3,1,0:T(8,128)(2,1)S(1)}, u32[]{:S(2)}, u32[]{:S(2)}) async-start(bf16[8,1,1024,112]{2,3,1,0:T(8,128)(2,1)} %bitcast.81), calls=%async_computation.3 | async-start | bytes 3670016 | tf_op jit(solution)/shard_map/all_to_all | solution.py:39
  144.4 8.9 %collective-permute-start = (bf16[1,1,1024,112]{2,3,1,0:T(8,128)(2,1)S(1)}, bf16[1,1,1024,112]{2,3,1,0:T(8,128)(2,1)S(1)}, u32[]{:S(2)}, u32[]{:S(2)}) collective-permute-start(bf16[1,1,1024,112]{2,3,1,0:T(8,128)(2,1)S(1)} %bitcast.84), channel_id=1, source_target_pairs={{0,8},{8,0},{16,24},{24,16},{32,40},{40,32},{48,56},{56,48},{64,72... | collective-permute-start | bytes 688136 | tf_op jit(solution)/shard_map/ppermute | solution.py:44
  166.0 1.9 copy-start
  167.9 27.9 %all-to-all-start.2 = ((bf16[8,1,1024,112]{2,3,1,0:T(8,128)(2,1)}), bf16[8,1,1024,112]{2,3,1,0:T(8,128)(2,1)S(1)}, u32[]{:S(2)}, u32[]{:S(2)}) async-start(bf16[8,1,1024,112]{2,3,1,0:T(8,128)(2,1)} %broadcast_in_dim.12), calls=%async_computation.2 | async-start | bytes 3670016 | tf_op jit(solution)/shard_map/all_to_all | solution.py:49
  174.2 8.9 %collective-permute-start.1 = (bf16[1,1,1024,112]{2,3,1,0:T(8,128)(2,1)S(1)}, bf16[1,1,1024,112]{2,3,1,0:T(8,128)(2,1)S(1)}, u32[]{:S(2)}, u32[]{:S(2)}) collective-permute-start(bf16[1,1,1024,112]{2,3,1,0:T(8,128)(2,1)S(1)} %bitcast.83), channel_id=1, source_target_pairs={{0,8},{8,0},{16,24},{24,16},{32,40},{40,32},{48,56},{56,48},{64,72... | collective-permute-start | bytes 688136 | tf_op jit(solution)/shard_map/ppermute | solution.py:44
  197.2 5.3 %copy-start.7 = (f32[8]{0:T(128)S(1)}, f32[8]{0:T(128)}, u32[]{:S(2)}) copy-start(f32[8]{0:T(128)} %param.8) | copy-start | bytes 100
  197.2 5.4 %copy-start.8 = (f32[32]{0:T(128)S(1)}, f32[32]{0:T(128)}, u32[]{:S(2)}) copy-start(f32[32]{0:T(128)} %param.7) | copy-start | bytes 388
  197.2 6.0 %copy-start.6 = (f32[1024]{0:T(1024)S(1)}, f32[1024]{0:T(1024)}, u32[]{:S(2)}) copy-start(f32[1024]{0:T(1024)} %param.9) | copy-start | bytes 12292
  197.2 28.8 %all-to-all-start.4 = ((bf16[8,1,1024,112]{2,3,1,0:T(8,128)(2,1)}), bf16[8,1,1024,112]{2,3,1,0:T(8,128)(2,1)}, u32[]{:S(2)}, u32[]{:S(2)}) async-start(bf16[8,1,1024,112]{2,3,1,0:T(8,128)(2,1)} %broadcast_in_dim.14), calls=%async_computation.4 | async-start | bytes 3670016 | tf_op jit(solution)/shard_map/all_to_all | solution.py:49
  206.5 23.4 %copy-start.3 = (bf16[4,128,1792]{1,0,2:T(4,128)(2,1)S(1)}, bf16[4,128,1792]{1,0,2:T(4,128)(2,1)}, u32[]{:S(2)}) copy-start(bf16[4,128,1792]{1,0,2:T(4,128)(2,1)} %copy-done.2) | copy-start | bytes 5505028
Sparse Core Ops, SparseCore 0:
  44.3 54.1 all-gather.2
where the time goes:
time: 245 us; the launch traced here: 244 us
  waiting for transfers between devices  118 us (48%)
  blocking collectives  37.6 us (15%)
  starting transfers between devices  35.9 us (15%)
  local copies, waits for them, and re-layouts  21 us (9%)
  matrix products  13.6 us (6%)
  between operations  13.5 us (6%)
  other arithmetic  4.48 us (2%)
    all_gather x1, waiting for transfers between devices, stacked_from(): pieces = lax.all_gather(pieces, axes[k], axis=0, tiled=True)  41 us
    all_gather x1, blocking collectives, stacked_from(): pieces = lax.all_gather(pieces, axes[k], axis=0, tiled=True)  37.6 us
    all_to_all x2, waiting for transfers between devices, from_everyone(): lax.all_to_all(jnp.broadcast_to(x[None], (devices, *x.shape)), axis, 0, 0...  32.1 us
    all_to_all x2, waiting for transfers between devices, sum_at_owner(): lax.all_to_all(pieces, axis, split_axis=0, concat_axis=0, tiled=True)  32.1 us
    ppermute x2, waiting for transfers between devices, from_partner(): lax.ppermute(x, axis, [(i, i ^ 1 << bit) for i in range(lax.axis_size(axi...  13.1 us
    all_to_all x1, starting transfers between devices, on_device(): lax.all_to_all(blocks, 'virt', split_axis=1, concat_axis=1, tiled=True)  11.7 us
    all_to_all x2, starting transfers between devices, from_everyone(): lax.all_to_all(jnp.broadcast_to(x[None], (devices, *x.shape)), axis, 0, 0...  9.77 us
    all_to_all x2, starting transfers between devices, sum_at_owner(): lax.all_to_all(pieces, axis, split_axis=0, concat_axis=0, tiled=True)  9.59 us
  transfers between devices with their start and end apart: 8, of which 7 were waited for; matrix products, arithmetic and copies ran while one was open for 7% of the time, Pallas kernels for 0%

commit v1 on v0

v1 whole, which is shorter than its diff:
```python
import jax
import jax.numpy as jnp
from jax import lax
from jax.experimental import pallas as pl
from jax.experimental.pallas import tpu as pltpu
from jax.sharding import PartitionSpec as P

MESH = pl.DeviceIdType.MESH
BF = jnp.bfloat16
F32 = jnp.float32
NZ, NX, NY = 16, 4, 4
TILE = 128
BLOCK = 112
SHARE = 28
CHUNKS = 8
FORMS = "EGEGEGEG"


def kernel(amp, vec, e_first, e_second, e_virtual, out,
           xg, lay, ltb, pbuf, b2, comb, tbuf, r1, s2, r2, inter, acc, away,
           xs, xr, ps, pr, ys, yr, zs, zr, cs, cr, g1s, g1r, g2s, g2r, g3s, g3r, g4s, g4r, os_, or_):
    p = lax.axis_index("pair")
    v = lax.axis_index("virt")
    z, x, y, c = p // NX, p % NX, v // 2, v % 2
    xo = x % 2
    xp = x + 1 - 2 * xo

    def dev(z=z, x=x, y=y, c=c):
        return (z * NX + x, y * 2 + c)

    core = dev(c=1 - c)
    across = dev(x=xp)
    y_up = [None] + [dev(y=(y + r) % NY) for r in range(1, NY)]
    y_down = [None] + [dev(y=(y + NY - r) % NY) for r in range(1, NY)]
    x_up = [None] + [dev(x=(x + r) % NX) for r in range(1, NX)]
    z_up = dev(z=(z + 1) % NZ)
    z_down = dev(z=(z + NZ - 1) % NZ)

    started = []

    def send(src, dst, ssem, rsem, target):
        copy = pltpu.make_async_remote_copy(
            src_ref=src, dst_ref=dst, send_sem=ssem, recv_sem=rsem, device_id=target, device_id_type=MESH
        )
        copy.start()
        started.append(copy)
        return copy

    barrier = pltpu.get_barrier_semaphore()
    partners = [core, *y_up[1:], *x_up[1:], z_up, z_down]
    for partner in partners:
        pl.semaphore_signal(barrier, inc=1, device_id=partner, device_id_type=MESH)
    pl.semaphore_wait(barrier, len(partners))

    x_copies = []
    for r in range(1, NX):
        to = (x + r) % NX
        x_copies.append(send(vec.at[to % 2], xg.at[x], xs.at[r - 1], xr.at[r - 1], x_up[r]))
    p_copy = send(amp.at[:, :, 1 - c], pbuf, ps.at[0], pr.at[0], core)
    y_copies = [None] * NY
    for r in (1, 3, 2):
        y_copies[r] = send(amp.at[:, (y + r) % NY], b2.at[r - 1], ys.at[r - 1], yr.at[r - 1], y_up[r])

    xg[x] = vec[xo]
    for copy in x_copies:
        copy.wait_recv()
    for j in range(4):
        for k in range(NX):
            lay[j, SHARE * k : SHARE * (k + 1), :] = xg[k].astype(F32)[SHARE * j : SHARE * (j + 1), :]
    for j in range(4):
        ltb[0, 0, j] = lay[j].astype(BF)

    z_copies = {}
    c_copies = {}

    def share(slot):
        for u in range(2):
            part = pl.ds(2 * u, 2)
            c_copies[slot, u] = send(
                ltb.at[slot, 0, part], ltb.at[slot, 1, part], cs.at[slot, u], cr.at[slot, u], core
            )

    def ring(step):
        for u in range(2):
            part = pl.ds(2 * u, 2)
            if step <= 8:
                z_copies[0, step, u] = send(
                    ltb.at[step - 1, 0, part], ltb.at[step, 0, part],
                    zs.at[0, step - 1, u], zr.at[0, step - 1, u], z_down,
                )
            if step <= 7:
                z_copies[1, step, u] = send(
                    ltb.at[(NZ + 1 - step) % NZ, 0, part], ltb.at[NZ - step, 0, part],
                    zs.at[1, step - 1, u], zr.at[1, step - 1, u], z_up,
                )

    def service(step):
        for u in range(2):
            for way in range(2):
                if (way, step, u) in z_copies:
                    z_copies[way, step, u].wait_recv()
        if step < 8:
            ring(step + 1)
        share(step)
        if step <= 7:
            share(NZ - step)

    ring(1)
    share(0)

    p_copy.wait_recv()

    def turn(r):
        at = (y + NY - r) % NY
        for l in range(4):
            for s in range(2):
                block = amp[l, at, c] if s == 0 else pbuf[l, at]
                comb[pl.ds((2 * l + s) * TILE, TILE), pl.ds(r * TILE, TILE)] = block.T

    def mirror(r):
        for l in range(4):
            for s in range(2):
                half = c if s == 0 else 1 - c
                rows, cols = pl.ds((2 * l + s) * TILE, TILE), pl.ds(r * TILE, TILE)
                other = amp[l, y, half] if r == 0 else b2[r - 1, l, half]
                comb[rows, cols] = (2.0 * comb[rows, cols].astype(F32) - other.astype(F32)).astype(BF)

    turn(0)
    turn(1)
    service(1)
    turn(2)
    turn(3)
    service(2)
    mirror(0)
    service(3)
    for r in (1, 3):
        y_copies[r].wait_recv()
        mirror(r)
    service(4)
    y_copies[2].wait_recv()
    mirror(2)

    def vectors_of(slot):
        return jnp.concatenate([ltb[slot, s, j] for j in range(4) for s in range(2)], axis=1)

    one, two, three, four = {}, {}, {}, {}

    def stage_one(k):
        slots = ((NZ - k) % NZ, k + 1)
        for slot in slots:
            for u in range(2):
                c_copies[slot, u].wait_recv()
        for half, slot in enumerate(slots):
            term = jnp.dot(vectors_of(slot), comb[...], preferred_element_type=F32).astype(BF)
            for r in range(NY):
                tbuf[k, half, r] = term[:, r * TILE : (r + 1) * TILE]
        if FORMS[k] == "E":
            one[k] = [send(tbuf.at[k, 1 - xo], r1.at[k, pl.ds(0, 4)], g1s.at[k, 0], g1r.at[k, 0], across)]
        else:
            one[k] = [
                send(tbuf.at[k, :, r], r1.at[k, pl.ds(2 * (r - 1), 2)], g1s.at[k, r - 1], g1r.at[k, r - 1], y_down[r])
                for r in range(1, NY)
            ]

    def stage_two(k):
        for copy in one[k]:
            copy.wait_recv()
        if FORMS[k] == "E":
            for r in (1, 2, 3, 0):
                s2[k, r] = (tbuf[k, xo, r].astype(F32) + r1[k, r].astype(F32)).astype(BF)
            two[k] = [
                send(s2.at[k, r], r2.at[k, r - 1], g2s.at[k, r - 1], g2r.at[k, r - 1], y_down[r])
                for r in range(1, NY)
            ]
        else:
            for h in range(2):
                total = tbuf[k, h, 0].astype(F32)
                for r in range(1, NY):
                    total = total + r1[k, 2 * (r - 1) + h].astype(F32)
                s2[k, h] = total.astype(BF)
            two[k] = [send(s2.at[k, 1 - xo], r2.at[k, 0], g2s.at[k, 0], g2r.at[k, 0], across)]

    def stage_three(k):
        for copy in two[k]:
            copy.wait_recv()
        if FORMS[k] == "E":
            total = s2[k, 0].astype(F32)
            for r in range(1, NY):
                total = total + r2[k, r - 1].astype(F32)
            inter[k, xo, 0] = total.astype(BF)
            three[k] = [
                send(inter.at[k, xo, 0], inter.at[k, xo, r], g3s.at[k, r - 1], g3r.at[k, r - 1], y_up[r])
                for r in range(1, NY)
            ]
        else:
            inter[k, xo, 0] = (s2[k, xo].astype(F32) + r2[k, 0].astype(F32)).astype(BF)
            three[k] = [send(inter.at[k, xo, 0], inter.at[k, xo, 0], g3s.at[k, 0], g3r.at[k, 0], across)]

    def stage_four(k):
        for copy in three[k]:
            copy.wait_recv()
        if FORMS[k] == "E":
            four[k] = [send(inter.at[k, xo], inter.at[k, xo], g4s.at[k, 0], g4r.at[k, 0], across)]
        else:
            four[k] = [
                send(inter.at[k, :, 0], inter.at[k, :, r], g4s.at[k, r - 1], g4r.at[k, r - 1], y_up[r])
                for r in range(1, NY)
            ]

    def finish(k):
        for copy in four[k]:
            copy.wait_recv()
        slots = ((NZ - k) % NZ, k + 1)
        pad = jnp.zeros((256 - 2 * BLOCK, TILE), BF)
        left = jnp.concatenate(
            [jnp.concatenate([inter[k, 0, r], inter[k, 1, r], pad], axis=0).T for r in range(NY)], axis=0
        )
        wide = jnp.zeros((256 - 2 * BLOCK, 8 * TILE), BF)
        right = jnp.concatenate([vectors_of(slots[0]), vectors_of(slots[1]), wide], axis=0)
        product = jnp.dot(left, right, preferred_element_type=F32)
        if k == 0:
            acc[...] = product
        else:
            acc[...] += product

    for tick in range(CHUNKS + 4):
        if 0 <= tick - 1 < CHUNKS:
            stage_two(tick - 1)
        if 0 <= tick - 2 < CHUNKS:
            stage_three(tick - 2)
        if 0 <= tick - 3 < CHUNKS:
            stage_four(tick - 3)
        if tick < CHUNKS:
            stage_one(tick)
        if 5 <= tick + 5 <= 8:
            service(tick + 5)
        if 0 <= tick - 4 < CHUNKS:
            finish(tick - 4)

    turned = e_virtual[...].T
    first = e_first[p // 2]
    sides = []
    for r in range(NY):
        at = (y + NY - r) % NY
        column = jnp.where(c == 0, turned[:, 0:1], turned[:, 1:2])
        for q in range(1, NY):
            choice = jnp.where(c == 0, turned[:, 2 * q : 2 * q + 1], turned[:, 2 * q + 1 : 2 * q + 2])
            column = jnp.where(at == q, choice, column)
        sides.append(column)
    o_copies = []
    for s in (1, 0):
        half = c if s == 0 else 1 - c
        tops = e_virtual[pl.ds(2 * y + half, 1), :]
        for l in range(4):
            second = e_second[4 * xo + l]
            for r in range(NY):
                at = (y + NY - r) % NY
                values = (amp[l, at, c] if s == 0 else pbuf[l, at]).astype(F32)
                term = acc[r * TILE : (r + 1) * TILE, (2 * l + s) * TILE : (2 * l + s + 1) * TILE]
                result = ((sides[r] + tops - first - second) * values + term).astype(BF)
                if s == 0:
                    out[l, at, c] = result
                else:
                    away[l, at] = result
            if s == 1:
                o_copies.append(send(away.at[l], out.at[l, :, c], os_.at[l], or_.at[l], core))
    for copy in o_copies:
        copy.wait_recv()
    for copy in started:
        copy.wait_send()


def on_device(amplitudes, cholesky, energy_first, energy_second, energy_virtual):
    amp = amplitudes.reshape(4, NY, 2, TILE, TILE)
    vec = jnp.transpose(cholesky, (0, 2, 1)).reshape(2, 4 * SHARE, TILE)
    vmem = pl.BlockSpec(memory_space=pltpu.VMEM)
    smem = pl.BlockSpec(memory_space=pltpu.SMEM)
    dma = pltpu.SemaphoreType.DMA
    scratch = [
        pltpu.VMEM((NX, 4 * SHARE, TILE), BF),
        pltpu.VMEM((4, BLOCK, TILE), F32),
        pltpu.VMEM((NZ, 2, 4, BLOCK, TILE), BF),
        pltpu.VMEM((4, NY, TILE, TILE), BF),
        pltpu.VMEM((NY - 1, 4, 2, TILE, TILE), BF),
        pltpu.VMEM((8 * TILE, NY * TILE), BF),
        pltpu.VMEM((CHUNKS, 2, NY, BLOCK, TILE), BF),
        pltpu.VMEM((CHUNKS, 6, BLOCK, TILE), BF),
        pltpu.VMEM((CHUNKS, 4, BLOCK, TILE), BF),
        pltpu.VMEM((CHUNKS, 3, BLOCK, TILE), BF),
        pltpu.VMEM((CHUNKS, 2, NY, BLOCK, TILE), BF),
        pltpu.VMEM((NY * TILE, 8 * TILE), F32),
        pltpu.VMEM((4, NY, TILE, TILE), BF),
        dma((3,)), dma((3,)), dma((1,)), dma((1,)), dma((3,)), dma((3,)),
        dma((2, 8, 2)), dma((2, 8, 2)), dma((NZ, 2)), dma((NZ, 2)),
        *[dma((CHUNKS, 3)) for _ in range(8)],
        dma((4,)), dma((4,)),
    ]
    result = pl.pallas_call(
        kernel,
        out_shape=jax.ShapeDtypeStruct(amp.shape, BF),
        in_specs=[vmem, vmem, smem, smem, vmem],
        out_specs=vmem,
        scratch_shapes=scratch,
        compiler_params=pltpu.CompilerParams(collective_id=0, has_side_effects=True, vmem_limit_bytes=48 << 20),
        name="cycle",
    )(amp, vec, energy_first, energy_second, energy_virtual.reshape(8, TILE))
    return result.reshape(amplitudes.shape)


def solution(mesh):
    placed = (P("pair", None, "virt"), P(None, "virt", "pair"), P(), P(), P())
    return jax.shard_map(
        on_device, mesh=mesh, in_specs=placed, out_specs=P("pair", None, "virt"), check_vma=False
    )
```

time: 245 us -> 100 us (0.41)
  waiting for transfers between devices: 118 us -> 0 us
  Pallas kernels: 0 us -> 96.5 us
  blocking collectives: 37.6 us -> 0 us
  starting transfers between devices: 35.9 us -> 0 us
  local copies, waits for them, and re-layouts: 21 us -> 3.69 us
  matrix products: 13.6 us -> 0 us
  between operations: 13.5 us -> 0.05 us
  other arithmetic: 4.48 us -> 0 us
    pallas_call x0 -> x1, Pallas kernels: none -> 96.5 us  [on_device(): pl.pallas_call(kernel, out_shape=jax.ShapeDtypeStruct(amp.shape, BF), in_...]
    all_to_all x5 -> x0, waiting for transfers between devices: 64.3 us -> none  [the longest x2 32.1 us: from_everyone(): lax.all_to_all(jnp.broadcast_to(x[None], (devices, *x.shape)), axis, 0, 0...]
    all_gather x1 -> x0, waiting for transfers between devices: 41 us -> none  [stacked_from(): pieces = lax.all_gather(pieces, axes[k], axis=0, tiled=True)]
    all_gather x1 -> x0, blocking collectives: 37.6 us -> none  [stacked_from(): pieces = lax.all_gather(pieces, axes[k], axis=0, tiled=True)]
    all_to_all x5 -> x0, starting transfers between devices: 31.1 us -> none  [the longest x1 11.7 us: on_device(): lax.all_to_all(blocks, 'virt', split_axis=1, concat_axis=1, tiled=True)]
    dot_general x3 -> x0, matrix products: 13.6 us -> none  [the longest x2 8.2 us: on_device(): jnp.einsum('ilad,ldq->iaq', combined, picked, preferred_element_type=jnp....]
    ppermute x2 -> x0, waiting for transfers between devices: 13.1 us -> none  [from_partner(): lax.ppermute(x, axis, [(i, i ^ 1 << bit) for i in range(lax.axis_size(axi...]
    reshape x3 -> x1, local copies, waits for them, and re-layouts: 7.36 us -> 0.02 us  [on_device(): vec = jnp.transpose(cholesky, (0, 2, 1)).reshape(2, 4 * SHARE, TILE)]
  transfers between devices with their start and end apart: 8 -> 0, of which waited for: 7 -> 0; matrix products, arithmetic and copies ran while one was open for 7% -> 0% of each run, Pallas kernels for 0% -> 0%
where the time goes in v1:
time: 100 us
  Pallas kernels  96.5 us (96%)
  local copies, waits for them, and re-layouts  3.69 us (4%)
    pallas_call x1, Pallas kernels, on_device(): pl.pallas_call(kernel, out_shape=jax.ShapeDtypeStruct(amp.shape, BF), in_...  96.5 us
    unnamed x9, local copies, waits for them, and re-layouts  2.84 us

profile of v1, /device:TPU:1, one launch (start us, length us, event | category | flops | bytes accessed | tf_op | source)
XLA Modules:
  0.0 100.3 jit_solution(12532612020156988522)
XLA Ops:
  0.0 0.8 copy.7
  0.8 0.0 copy-start.1
  0.8 0.0 copy-start.2
  0.9 0.0 copy-start.3
  0.9 0.6 copy-done.1
  1.5 0.0 copy-done.2
  1.5 0.0 copy-done.3
  1.5 0.0 copy-start
  1.5 1.2 %copy-done = bf16[4,1024,128]{2,1,0:T(8,128)(2,1)S(1)} copy-done((bf16[4,1024,128]{2,1,0:T(8,128)(2,1)S(1)}, bf16[4,1024,128]{2,1,0:T(8,128)(2,1)}, u32[]{:S(2)}) %copy-start) | copy-done | bytes 1048600
  2.8 96.5 %cycle.1 = bf16[4,4,2,128,128]{4,3,2,1,0:T(8,128)(2,1)S(1)} custom-call(bf16[4,4,2,128,128]{4,3,2,1,0:T(8,128)(2,1)S(1)} %bitcast.5, bf16[2,112,128]{2,1,0:T(8,128)(2,1)S(1)} %reshape.13.vec, f32[32]{0:T(128)S(1)} %copy-done.2, f32[8]{0:T(128)S(1)} %copy-done.3, f32[8,128]{1,0:T(8,128)S(1)} %bitcast.6), custom_call_target="tpu_custom_call" | custom-call | tf_op jit(solution)/shard_map/cycle/pallas_call | solution.py:298
  99.3 1.0 copy.9
  (1 shorter events, 0.0 us)
Async XLA Ops:
  0.8 0.7 copy-start.1
  0.8 0.7 copy-start.2
  0.9 0.7 copy-start.3
  1.5 1.2 %copy-start = (bf16[4,1024,128]{2,1,0:T(8,128)(2,1)S(1)}, bf16[4,1024,128]{2,1,0:T(8,128)(2,1)}, u32[]{:S(2)}) copy-start(bf16[4,1024,128]{2,1,0:T(8,128)(2,1)} %param.5) | copy-start | bytes 3145732

commit v2 on v1

v2 whole, which is shorter than its diff:
```python
import jax
import jax.numpy as jnp
from jax import lax
from jax.experimental import pallas as pl
from jax.experimental.pallas import tpu as pltpu
from jax.sharding import PartitionSpec as P

MESH = pl.DeviceIdType.MESH
BF = jnp.bfloat16
F32 = jnp.float32
NZ, NX, NY = 16, 4, 4
TILE = 128
BLOCK = 112
SHARE = 28
CHUNKS = 8
FORMS = "EGEGEGDD"
ROWS = ((0, 64), (64, 48))
LAG = 3


def kernel(amp, vec, e_first, e_second, e_virtual, out,
           own, tops_of, xg, lay, ltb, pbuf, b2, comb, tbuf, r1, s2, r2, inter, acc, away,
           lsem, xs, xr, ps, pr, ys, yr, zs, zr, cs, cr, gs, gr, os_, or_):
    p = lax.axis_index("pair")
    v = lax.axis_index("virt")
    z, x, y, c = p // NX, p % NX, v // 2, v % 2
    xo = x % 2
    xp = x + 1 - 2 * xo

    def dev(z=z, x=x, y=y, c=c):
        return (z * NX + x, y * 2 + c)

    core = dev(c=1 - c)
    across = dev(x=xp)
    y_up = [None] + [dev(y=(y + r) % NY) for r in range(1, NY)]
    y_down = [None] + [dev(y=(y + NY - r) % NY) for r in range(1, NY)]
    x_up = [None] + [dev(x=(x + r) % NX) for r in range(1, NX)]
    z_up = dev(z=(z + 1) % NZ)
    z_down = dev(z=(z + NZ - 1) % NZ)

    y_slant = [across] + [dev(x=xp, y=(y + r) % NY) for r in range(1, NY)]
    y_slope = [across] + [dev(x=xp, y=(y + NY - r) % NY) for r in range(1, NY)]

    def send(src, dst, ssem, rsem, target):
        copy = pltpu.make_async_remote_copy(
            src_ref=src, dst_ref=dst, send_sem=ssem, recv_sem=rsem, device_id=target, device_id_type=MESH
        )
        copy.start()
        return copy

    def whole(ref, ssem, rsem):
        return pltpu.make_async_remote_copy(
            src_ref=ref, dst_ref=ref, send_sem=ssem, recv_sem=rsem, device_id=core, device_id_type=MESH
        )

    local = [
        pltpu.make_async_copy(amp, own, lsem.at[0]),
        pltpu.make_async_copy(e_virtual, tops_of, lsem.at[1]),
    ]
    for copy in local:
        copy.start()

    barrier = pltpu.get_barrier_semaphore()
    partners = [core, *y_up[1:], *x_up[1:], z_up, z_down, *y_slant[1:]]

    def enter():
        for partner in partners:
            pl.semaphore_signal(barrier, inc=1, device_id=partner, device_id_type=MESH)
        pl.semaphore_wait(barrier, len(partners))

    enter()

    for r in range(1, NX):
        to = (x + r) % NX
        send(vec.at[to % 2], xg.at[x], xs.at[0], xr.at[0], x_up[r])
    p_copy = send(amp.at[:, :, 1 - c], pbuf, ps.at[0], pr.at[0], core)
    y_copies = [None] * NY
    for r in (1, 3, 2):
        y_copies[r] = send(amp.at[:, (y + r) % NY], b2.at[r - 1], ys.at[0], yr.at[r - 1], y_up[r])
    xg[x] = vec[xo]
    x_all = whole(xg.at[pl.ds(0, NX - 1)], xs.at[0], xr.at[0])
    y_all = whole(b2, ys.at[0], yr.at[0])

    def arrive(copies):
        for copy in copies:
            copy.wait_recv()

    def spread():
        for j in range(4):
            for k in range(NX):
                lay[j, SHARE * k : SHARE * (k + 1), :] = xg[k].astype(F32)[SHARE * j : SHARE * (j + 1), :]

    arrive([x_all])
    spread()

    z_copies = {}
    pending = {}

    def settle(key):
        if key in pending:
            pending.pop(key).wait_send()

    def share(way, step, u):
        slot = step if way == 0 else NZ - step
        key = ("c", way, step % 2)
        if u == 0:
            settle(key)
        sem = cs.at[way, step % 2]
        send(ltb.at[slot, 0, u], ltb.at[slot, 1, u], sem, cr.at[slot], core)
        pending[key] = whole(ltb.at[slot, 0], sem, cr.at[slot])

    def ring(step, way, u):
        if step > 8 - way:
            return
        source = step - 1 if way == 0 else (NZ + 1 - step) % NZ
        target = step if way == 0 else NZ - step
        key = ("z", way, step % 2)
        if u == 0:
            settle(key)
        sem = zs.at[way, step % 2]
        z_copies[way, step, u] = send(
            ltb.at[source, 0, u], ltb.at[target, 0, u], sem, zr.at[way, step - 1, u], z_up if way else z_down
        )
        pending[key] = whole(ltb.at[source, 0], sem, zr.at[way, step - 1, u])

    def relay(step, u):
        for way in range(2):
            if (way, step, u) in z_copies:
                z_copies[way, step, u].wait_recv()
                ring(step + 1, way, u)
                share(way, step, u)

    def service(step):
        for u in range(4):
            relay(step, u)

    for j in range(4):
        ltb[0, 0, j] = lay[j].astype(BF)
        ring(1, 0, j)
        ring(1, 1, j)
        share(0, 0, j)

    for copy in local:
        copy.wait()
    arrive([p_copy])

    def turn(r):
        at = (y + NY - r) % NY
        for l in range(4):
            for s in range(2):
                block = own[l, at, c] if s == 0 else pbuf[l, at]
                comb[pl.ds((2 * l + s) * TILE, TILE), pl.ds(r * TILE, TILE)] = block.T

    def mirror(r):
        for l in range(4):
            for s in range(2):
                half = c if s == 0 else 1 - c
                rows, cols = pl.ds((2 * l + s) * TILE, TILE), pl.ds(r * TILE, TILE)
                other = own[l, y, half] if r == 0 else b2[r - 1, l, half]
                comb[rows, cols] = (2.0 * comb[rows, cols].astype(F32) - other.astype(F32)).astype(BF)

    turn(0)
    turn(1)
    service(1)
    turn(2)
    turn(3)
    mirror(0)
    service(2)
    for r in (1, 3, 2):
        arrive([y_copies[r]])
        mirror(r)

    def vectors_of(slot):
        return jnp.concatenate([ltb[slot, s, j] for j in range(4) for s in range(2)], axis=1)

    landed = {}

    def post(stage, n, region, copies):
        key = (stage, n % 4)
        settle(key)
        ssem, rsem = gs.at[stage, n % 4], gr.at[stage, n]
        for src, dst, target in copies:
            send(src, dst, ssem, rsem, target)
        pending[key] = landed[stage, n] = whole(region, ssem, rsem)

    def rows_of(n):
        return n // 2, pl.ds(*ROWS[n % 2])

    def stage_one(k):
        slots = ((NZ - k) % NZ, k + 1)
        for slot in slots:
            whole(ltb.at[slot, 1], cs.at[0, 0], cr.at[slot]).wait_recv()
        for half, slot in enumerate(slots):
            term = jnp.dot(vectors_of(slot), comb[...], preferred_element_type=F32).astype(BF)
            for r in range(NY):
                tbuf[k, half, r] = term[:, r * TILE : (r + 1) * TILE]
        for n in (2 * k, 2 * k + 1):
            _, rows = rows_of(n)
            if FORMS[k] == "E":
                post(0, n, r1.at[k, pl.ds(0, 4), rows],
                     [(tbuf.at[k, 1 - xo, :, rows], r1.at[k, pl.ds(0, 4), rows], across)])
            elif FORMS[k] == "G":
                post(0, n, r1.at[k, pl.ds(0, 6), rows],
                     [(tbuf.at[k, :, r, rows], r1.at[k, pl.ds(2 * (r - 1), 2), rows], y_down[r]) for r in (2, 1, 3)])
            else:
                post(0, n, r1.at[k, :, rows],
                     [(tbuf.at[k, 1 - xo, r, rows], r1.at[k, 3 + r, rows], y_slope[r]) for r in (2, 1, 3, 0)]
                     + [(tbuf.at[k, xo, r, rows], r1.at[k, r - 1, rows], y_down[r]) for r in (2, 1, 3)])

    def stage_two(n):
        k, rows = rows_of(n)
        landed[0, n].wait_recv()
        if FORMS[k] == "E":
            for r in range(NY):
                s2[k, r, rows] = (tbuf[k, xo, r, rows].astype(F32) + r1[k, r, rows].astype(F32)).astype(BF)
            post(1, n, r2.at[k, :, rows],
                 [(s2.at[k, r, rows], r2.at[k, r - 1, rows], y_down[r]) for r in (2, 1, 3)])
        elif FORMS[k] == "G":
            for h in range(2):
                total = tbuf[k, h, 0, rows].astype(F32)
                for r in range(1, NY):
                    total = total + r1[k, 2 * (r - 1) + h, rows].astype(F32)
                s2[k, h, rows] = total.astype(BF)
            post(1, n, r2.at[k, 0, rows], [(s2.at[k, 1 - xo, rows], r2.at[k, 0, rows], across)])
        else:
            total = tbuf[k, xo, 0, rows].astype(F32)
            for q in range(7):
                total = total + r1[k, q, rows].astype(F32)
            inter[k, xo, 0, rows] = total.astype(BF)
            mine = inter.at[k, xo, 0, rows]
            post(3, n, inter.at[k, 1 - xo, :, rows],
                 [(mine, inter.at[k, xo, r, rows], y_slant[r]) for r in (2, 1, 3, 0)])
            post(2, n, inter.at[k, xo, pl.ds(1, 3), rows],
                 [(mine, inter.at[k, xo, r, rows], y_up[r]) for r in (2, 1, 3)])

    def stage_three(n):
        k, rows = rows_of(n)
        landed[1, n].wait_recv()
        if FORMS[k] == "E":
            total = s2[k, 0, rows].astype(F32)
            for r in range(1, NY):
                total = total + r2[k, r - 1, rows].astype(F32)
            inter[k, xo, 0, rows] = total.astype(BF)
            post(2, n, inter.at[k, xo, pl.ds(1, 3), rows],
                 [(inter.at[k, xo, 0, rows], inter.at[k, xo, r, rows], y_up[r]) for r in (2, 1, 3)])
        else:
            inter[k, xo, 0, rows] = (s2[k, xo, rows].astype(F32) + r2[k, 0, rows].astype(F32)).astype(BF)
            post(2, n, inter.at[k, 1 - xo, 0, rows],
                 [(inter.at[k, xo, 0, rows], inter.at[k, xo, 0, rows], across)])

    def stage_four(n):
        k, rows = rows_of(n)
        landed[2, n].wait_recv()
        if FORMS[k] == "E":
            post(3, n, inter.at[k, 1 - xo, :, rows],
                 [(inter.at[k, xo, :, rows], inter.at[k, xo, :, rows], across)])
        else:
            post(3, n, inter.at[k, :, pl.ds(1, 3), rows],
                 [(inter.at[k, :, 0, rows], inter.at[k, :, r, rows], y_up[r]) for r in (2, 1, 3)])

    def finish(k):
        for n in (2 * k, 2 * k + 1):
            if FORMS[k] == "D":
                landed[2, n].wait_recv()
            landed[3, n].wait_recv()
        slots = ((NZ - k) % NZ, k + 1)
        pad = jnp.zeros((256 - 2 * BLOCK, TILE), BF)
        left = jnp.concatenate(
            [jnp.concatenate([inter[k, 0, r], inter[k, 1, r], pad], axis=0).T for r in range(NY)], axis=0
        )
        wide = jnp.zeros((256 - 2 * BLOCK, 8 * TILE), BF)
        right = jnp.concatenate([vectors_of(slots[0]), vectors_of(slots[1]), wide], axis=0)
        product = jnp.dot(left, right, preferred_element_type=F32)
        if k == 0:
            acc[...] = product
        else:
            acc[...] += product

    plan = []
    for step in range(3, 9):
        for u in range(4):
            plan.append((2 * (step - 2) + 0.5 * u - 0.3, 9, relay, (step, u)))
    for k in range(CHUNKS):
        short = FORMS[k] == "D"
        plan.append((2 * k, 4, stage_one, (k,)))
        for n in (2 * k, 2 * k + 1):
            plan.append((n + LAG, 3, stage_two, (n,)))
            if not short:
                plan.append((n + 2 * LAG, 2, stage_three, (n,)))
                plan.append((n + 3 * LAG, 1, stage_four, (n,)))
        plan.append((2 * k + 1 + (2 if short else 4) * LAG, 5, finish, (k,)))
    for _, _, act, what in sorted(plan, key=lambda item: item[:2]):
        act(*what)

    def conclude():
        turned = tops_of[...].T
        first = e_first[p // 2]
        sides = []
        for r in range(NY):
            at = (y + NY - r) % NY
            column = jnp.where(c == 0, turned[:, 0:1], turned[:, 1:2])
            for q in range(1, NY):
                choice = jnp.where(c == 0, turned[:, 2 * q : 2 * q + 1], turned[:, 2 * q + 1 : 2 * q + 2])
                column = jnp.where(at == q, choice, column)
            sides.append(column)
        for s in (1, 0):
            half = c if s == 0 else 1 - c
            tops = tops_of[pl.ds(2 * y + half, 1), :]
            for l in range(4):
                second = e_second[4 * xo + l]
                for r in range(NY):
                    at = (y + NY - r) % NY
                    values = (own[l, at, c] if s == 0 else pbuf[l, at]).astype(F32)
                    term = acc[r * TILE : (r + 1) * TILE, (2 * l + s) * TILE : (2 * l + s + 1) * TILE]
                    result = ((sides[r] + tops - first - second) * values + term).astype(BF)
                    if s == 0:
                        out[l, at, c] = result
                    else:
                        away[l, at] = result
                if s == 1:
                    send(away.at[l], out.at[l, :, c], os_.at[0], or_.at[0], core)

    conclude()
    last = whole(away, os_.at[0], or_.at[0])
    arrive([last])

    def drain():
        for copy in (x_all, p_copy, y_all, last, *pending.values()):
            copy.wait_send()

    drain()


def on_device(amplitudes, cholesky, energy_first, energy_second, energy_virtual):
    amp = amplitudes.reshape(4, NY, 2, TILE, TILE)
    vec = jnp.transpose(cholesky, (0, 2, 1)).reshape(2, 4 * SHARE, TILE)
    vmem = pl.BlockSpec(memory_space=pltpu.VMEM)
    hbm = pl.BlockSpec(memory_space=pltpu.HBM)
    smem = pl.BlockSpec(memory_space=pltpu.SMEM)
    dma = pltpu.SemaphoreType.DMA
    scratch = [
        pltpu.VMEM((4, NY, 2, TILE, TILE), BF),
        pltpu.VMEM((8, TILE), F32),
        pltpu.VMEM((NX, 4 * SHARE, TILE), BF),
        pltpu.VMEM((4, BLOCK, TILE), F32),
        pltpu.VMEM((NZ, 2, 4, BLOCK, TILE), BF),
        pltpu.VMEM((4, NY, TILE, TILE), BF),
        pltpu.VMEM((NY - 1, 4, 2, TILE, TILE), BF),
        pltpu.VMEM((8 * TILE, NY * TILE), BF),
        pltpu.VMEM((CHUNKS, 2, NY, BLOCK, TILE), BF),
        pltpu.VMEM((CHUNKS, 7, BLOCK, TILE), BF),
        pltpu.VMEM((CHUNKS, 4, BLOCK, TILE), BF),
        pltpu.VMEM((CHUNKS, 3, BLOCK, TILE), BF),
        pltpu.VMEM((CHUNKS, 2, NY, BLOCK, TILE), BF),
        pltpu.VMEM((NY * TILE, 8 * TILE), F32),
        pltpu.VMEM((4, NY, TILE, TILE), BF),
        dma((2,)), dma((1,)), dma((1,)), dma((1,)), dma((1,)), dma((1,)), dma((3,)),
        dma((2, 2)), dma((2, 8, 4)), dma((2, 2)), dma((NZ,)),
        dma((4, 4)), dma((4, 2 * CHUNKS)), dma((1,)), dma((1,)),
    ]
    result = pl.pallas_call(
        kernel,
        out_shape=jax.ShapeDtypeStruct(amp.shape, BF),
        in_specs=[hbm, vmem, smem, smem, hbm],
        out_specs=vmem,
        scratch_shapes=scratch,
        compiler_params=pltpu.CompilerParams(collective_id=0, has_side_effects=True, vmem_limit_bytes=48 << 20),
        name="cycle",
    )(amp, vec, energy_first, energy_second, energy_virtual.reshape(8, TILE))
    return result.reshape(amplitudes.shape)


def solution(mesh):
    placed = (P("pair", None, "virt"), P(None, "virt", "pair"), P(), P(), P())
    return jax.shard_map(
        on_device, mesh=mesh, in_specs=placed, out_specs=P("pair", None, "virt"), check_vma=False
    )
```

time: 100 us -> 76.8 us (0.77)
  Pallas kernels: 96.5 us -> 72.8 us
    pallas_call x1, Pallas kernels: 96.5 us -> 72.8 us  [on_device(): pl.pallas_call(kernel, out_shape=jax.ShapeDtypeStruct(amp.shape, BF), in_...]
where the time goes in v2:
time: 76.8 us; the launch traced here: 76.5 us
  Pallas kernels  72.8 us (95%)
  local copies, waits for them, and re-layouts  3.69 us (5%)
    pallas_call x1, Pallas kernels, on_device(): pl.pallas_call(kernel, out_shape=jax.ShapeDtypeStruct(amp.shape, BF), in_...  72.8 us
    unnamed x9, local copies, waits for them, and re-layouts  2.84 us

profile of v2, /device:TPU:1, one launch (start us, length us, event | category | flops | bytes accessed | tf_op | source)
XLA Modules:
  0.0 76.5 jit_solution(18202600941403194448)
XLA Ops:
  0.0 0.8 %copy.7 = bf16[8,28,128]{2,1,0:T(8,128)(2,1)S(1)} copy(bf16[8,28,128]{2,0,1:T(8,128)(2,1)} %bitcast.7) | data formatting | bytes 114688 | tf_op jit(solution)/shard_map/transpose | solution.py:336
  0.8 0.0 copy-start.1
  0.8 0.0 copy-start.2
  0.9 0.0 copy-start.3
  0.9 0.6 copy-done.1
  1.5 0.0 copy-done.2
  1.5 0.0 copy-done.3
  1.5 0.0 copy-start
  1.5 1.2 %copy-done = bf16[4,1024,128]{2,1,0:T(8,128)(2,1)S(1)} copy-done((bf16[4,1024,128]{2,1,0:T(8,128)(2,1)S(1)}, bf16[4,1024,128]{2,1,0:T(8,128)(2,1)}, u32[]{:S(2)}) %copy-start) | copy-done | bytes 1048600
  2.8 72.8 %cycle.1 = bf16[4,4,2,128,128]{4,3,2,1,0:T(8,128)(2,1)S(1)} custom-call(bf16[4,4,2,128,128]{4,3,2,1,0:T(8,128)(2,1)S(1)} %bitcast.5, bf16[2,112,128]{2,1,0:T(8,128)(2,1)S(1)} %reshape.13.vec, f32[32]{0:T(128)S(1)} %copy-done.2, f32[8]{0:T(128)S(1)} %copy-done.3, f32[8,128]{1,0:T(8,128)S(1)} %bitcast.6), custom_call_target="tpu_custom_call" | custom-call | tf_op jit(solution)/shard_map/cycle/pallas_call | solution.py:361
  75.6 1.0 %copy.9 = bf16[4,1024,128]{2,1,0:T(8,128)(2,1)} copy(bf16[4,1024,128]{2,1,0:T(8,128)(2,1)S(1)} %bitcast.4) | data formatting | bytes 2097152
  (1 shorter events, 0.0 us)
Async XLA Ops:
  0.8 0.7 copy-start.1
  0.8 0.7 copy-start.2
  0.9 0.7 copy-start.3
  1.5 1.2 %copy-start = (bf16[4,1024,128]{2,1,0:T(8,128)(2,1)S(1)}, bf16[4,1024,128]{2,1,0:T(8,128)(2,1)}, u32[]{:S(2)}) copy-start(bf16[4,1024,128]{2,1,0:T(8,128)(2,1)} %param.5) | copy-start | bytes 3145732

commit v3 on v2

--- a/solution.py
+++ b/solution.py
@@ -13,13 +13,14 @@
 BLOCK = 112
 SHARE = 28
 CHUNKS = 8
-FORMS = "EGEGEGDD"
+FORMS = "EEGEEGED"
 ROWS = ((0, 64), (64, 48))
 LAG = 3
-
-
-def kernel(amp, vec, e_first, e_second, e_virtual, out,
-           own, tops_of, xg, lay, ltb, pbuf, b2, comb, tbuf, r1, s2, r2, inter, acc, away,
+GRANT = 66_900_000
+
+
+def kernel(amp, chol, first_hbm, second_hbm, virtual_hbm, out,
+           own, tops_of, e_first, e_second, raw, wide_raw, flat, vec, xg, lay, ltb, pbuf, b2, comb, tbuf, r1, s2, r2, inter, acc, away, keep,
            lsem, xs, xr, ps, pr, ys, yr, zs, zr, cs, cr, gs, gr, os_, or_):
     p = lax.axis_index("pair")
     v = lax.axis_index("virt")
@@ -55,8 +56,12 @@
 
     local = [
         pltpu.make_async_copy(amp, own, lsem.at[0]),
-        pltpu.make_async_copy(e_virtual, tops_of, lsem.at[1]),
+        pltpu.make_async_copy(virtual_hbm, tops_of, lsem.at[1]),
+        pltpu.make_async_copy(first_hbm, e_first, lsem.at[2]),
+        pltpu.make_async_copy(second_hbm, e_second, lsem.at[3]),
     ]
+    chol_copy = pltpu.make_async_copy(chol, raw, lsem.at[4])
+    chol_copy.start()
     for copy in local:
         copy.start()
 
@@ -66,6 +71,13 @@
     def enter():
         for partner in partners:
             pl.semaphore_signal(barrier, inc=1, device_id=partner, device_id_type=MESH)
+        chol_copy.wait()
+        wide_raw[...] = raw[...].astype(F32)
+        for j in range(4):
+            for g in range(2):
+                flat[g, SHARE * j : SHARE * (j + 1), :] = wide_raw[:, 4 * g + j, :]
+        for g in range(2):
+            vec[g] = flat[g].astype(BF)
         pl.semaphore_wait(barrier, len(partners))
 
     enter()
@@ -314,10 +326,12 @@
                     term = acc[r * TILE : (r + 1) * TILE, (2 * l + s) * TILE : (2 * l + s + 1) * TILE]
                     result = ((sides[r] + tops - first - second) * values + term).astype(BF)
                     if s == 0:
-                        out[l, at, c] = result
+                        keep[l, at] = result
                     else:
                         away[l, at] = result
-                if s == 1:
+                if s == 0:
+                    pltpu.make_async_copy(keep.at[l], out.at[l, :, c], lsem.at[5 + l]).start()
+                else:
                     send(away.at[l], out.at[l, :, c], os_.at[0], or_.at[0], core)
 
     conclude()
@@ -325,6 +339,8 @@
     arrive([last])
 
     def drain():
+        for l in range(4):
+            pltpu.make_async_copy(keep.at[l], out.at[l, :, c], lsem.at[5 + l]).wait()
         for copy in (x_all, p_copy, y_all, last, *pending.values()):
             copy.wait_send()
 
@@ -333,14 +349,19 @@
 
 def on_device(amplitudes, cholesky, energy_first, energy_second, energy_virtual):
     amp = amplitudes.reshape(4, NY, 2, TILE, TILE)
-    vec = jnp.transpose(cholesky, (0, 2, 1)).reshape(2, 4 * SHARE, TILE)
+    chol = jnp.transpose(cholesky, (2, 0, 1))
     vmem = pl.BlockSpec(memory_space=pltpu.VMEM)
     hbm = pl.BlockSpec(memory_space=pltpu.HBM)
-    smem = pl.BlockSpec(memory_space=pltpu.SMEM)
     dma = pltpu.SemaphoreType.DMA
     scratch = [
         pltpu.VMEM((4, NY, 2, TILE, TILE), BF),
         pltpu.VMEM((8, TILE), F32),
+        pltpu.SMEM((32,), F32),
+        pltpu.SMEM((8,), F32),
+        pltpu.VMEM((SHARE, 8, TILE), BF),
+        pltpu.VMEM((SHARE, 8, TILE), F32),
+        pltpu.VMEM((2, 4 * SHARE, TILE), F32),
+        pltpu.VMEM((2, 4 * SHARE, TILE), BF),
         pltpu.VMEM((NX, 4 * SHARE, TILE), BF),
         pltpu.VMEM((4, BLOCK, TILE), F32),
         pltpu.VMEM((NZ, 2, 4, BLOCK, TILE), BF),
@@ -354,19 +375,20 @@
         pltpu.VMEM((CHUNKS, 2, NY, BLOCK, TILE), BF),
         pltpu.VMEM((NY * TILE, 8 * TILE), F32),
         pltpu.VMEM((4, NY, TILE, TILE), BF),
-        dma((2,)), dma((1,)), dma((1,)), dma((1,)), dma((1,)), dma((1,)), dma((3,)),
+        pltpu.VMEM((4, NY, TILE, TILE), BF),
+        dma((9,)), dma((1,)), dma((1,)), dma((1,)), dma((1,)), dma((1,)), dma((3,)),
         dma((2, 2)), dma((2, 8, 4)), dma((2, 2)), dma((NZ,)),
         dma((4, 4)), dma((4, 2 * CHUNKS)), dma((1,)), dma((1,)),
     ]
     result = pl.pallas_call(
         kernel,
         out_shape=jax.ShapeDtypeStruct(amp.shape, BF),
-        in_specs=[hbm, vmem, smem, smem, hbm],
-        out_specs=vmem,
+        in_specs=[hbm] * 5,
+        out_specs=hbm,
         scratch_shapes=scratch,
-        compiler_params=pltpu.CompilerParams(collective_id=0, has_side_effects=True, vmem_limit_bytes=48 << 20),
+        compiler_params=pltpu.CompilerParams(collective_id=0, has_side_effects=True, vmem_limit_bytes=GRANT),
         name="cycle",
-    )(amp, vec, energy_first, energy_second, energy_virtual.reshape(8, TILE))
+    )(amp, chol, energy_first, energy_second, energy_virtual.reshape(8, TILE))
     return result.reshape(amplitudes.shape)
 
 

time: 76.8 us -> 74.7 us (0.973)
  local copies, waits for them, and re-layouts: 3.69 us -> 2.26 us
    transpose x1 -> x0, local copies, waits for them, and re-layouts: 0.83 us -> none  [on_device(): vec = jnp.transpose(cholesky, (0, 2, 1)).reshape(2, 4 * SHARE, TILE)]
    unnamed x9 -> x1, local copies, waits for them, and re-layouts: 2.84 us -> 2.26 us
where the time goes in v3:
time: 74.7 us; the launch traced here: 74.5 us
  Pallas kernels  72.2 us (97%)
  local copies, waits for them, and re-layouts  2.26 us (3%)
    pallas_call x1, Pallas kernels, on_device(): pl.pallas_call(kernel, out_shape=jax.ShapeDtypeStruct(amp.shape, BF), in_...  72.2 us
    unnamed x1, local copies, waits for them, and re-layouts  2.26 us

profile of v3, /device:TPU:1, one launch (start us, length us, event | category | flops | bytes accessed | tf_op | source)
XLA Modules:
  0.0 74.5 jit_solution(9171288422596269985)
XLA Ops:
  0.0 72.2 %cycle.1 = bf16[4,4,2,128,128]{4,3,2,1,0:T(8,128)(2,1)} custom-call(bf16[4,4,2,128,128]{4,3,2,1,0:T(8,128)(2,1)} %bitcast.5, bf16[28,8,128]{2,1,0:T(8,128)(2,1)} %bitcast.6, f32[32]{0:T(128)} %first_hbm.1, f32[8]{0:T(128)} %second_hbm.1, f32[8,128]{1,0:T(8,128)} %bitcast.7), custom_call_target="tpu_custom_call" | custom-call | tf_op jit(solution)/shard_map/cycle/pallas_call | solution.py:383
  72.2 2.3 %copy.7 = bf16[4,1024,128]{2,1,0:T(8,128)(2,1)} copy(bf16[4,1024,128]{2,1,0:T(8,128)(2,1)} %bitcast.4) | data formatting | bytes 2097152

commit v4 on v3

--- a/solution.py
+++ b/solution.py
@@ -16,11 +16,11 @@
 FORMS = "EEGEEGED"
 ROWS = ((0, 64), (64, 48))
 LAG = 3
-GRANT = 66_900_000
+GRANT = 48 << 20
 
 
 def kernel(amp, chol, first_hbm, second_hbm, virtual_hbm, out,
-           own, tops_of, e_first, e_second, raw, wide_raw, flat, vec, xg, lay, ltb, pbuf, b2, comb, tbuf, r1, s2, r2, inter, acc, away, keep,
+           own, tops_of, e_first, e_second, raw, wide_raw, flat, vec, xg, lay, ltb, pbuf, b2, comb, tbuf, r1, s2, r2, inter, acc, away,
            lsem, xs, xr, ps, pr, ys, yr, zs, zr, cs, cr, gs, gr, os_, or_):
     p = lax.axis_index("pair")
     v = lax.axis_index("virt")
@@ -326,12 +326,10 @@
                     term = acc[r * TILE : (r + 1) * TILE, (2 * l + s) * TILE : (2 * l + s + 1) * TILE]
                     result = ((sides[r] + tops - first - second) * values + term).astype(BF)
                     if s == 0:
-                        keep[l, at] = result
+                        out[l, at, c] = result
                     else:
                         away[l, at] = result
-                if s == 0:
-                    pltpu.make_async_copy(keep.at[l], out.at[l, :, c], lsem.at[5 + l]).start()
-                else:
+                if s == 1:
                     send(away.at[l], out.at[l, :, c], os_.at[0], or_.at[0], core)
 
     conclude()
@@ -339,8 +337,6 @@
     arrive([last])
 
     def drain():
-        for l in range(4):
-            pltpu.make_async_copy(keep.at[l], out.at[l, :, c], lsem.at[5 + l]).wait()
         for copy in (x_all, p_copy, y_all, last, *pending.values()):
             copy.wait_send()
 
@@ -375,8 +371,7 @@
         pltpu.VMEM((CHUNKS, 2, NY, BLOCK, TILE), BF),
         pltpu.VMEM((NY * TILE, 8 * TILE), F32),
         pltpu.VMEM((4, NY, TILE, TILE), BF),
-        pltpu.VMEM((4, NY, TILE, TILE), BF),
-        dma((9,)), dma((1,)), dma((1,)), dma((1,)), dma((1,)), dma((1,)), dma((3,)),
+        dma((5,)), dma((1,)), dma((1,)), dma((1,)), dma((1,)), dma((1,)), dma((3,)),
         dma((2, 2)), dma((2, 8, 4)), dma((2, 2)), dma((NZ,)),
         dma((4, 4)), dma((4, 2 * CHUNKS)), dma((1,)), dma((1,)),
     ]
@@ -384,11 +379,12 @@
         kernel,
         out_shape=jax.ShapeDtypeStruct(amp.shape, BF),
         in_specs=[hbm] * 5,
-        out_specs=hbm,
+        out_specs=vmem,
         scratch_shapes=scratch,
         compiler_params=pltpu.CompilerParams(collective_id=0, has_side_effects=True, vmem_limit_bytes=GRANT),
         name="cycle",
-    )(amp, chol, energy_first, energy_second, energy_virtual.reshape(8, TILE))
+    )(*[pltpu.with_memory_space_constraint(a, pltpu.HBM)
+        for a in (amp, chol, energy_first, energy_second, energy_virtual.reshape(8, TILE))])
     return result.reshape(amplitudes.shape)
 
 

time: 74.7 us -> 73.2 us (0.980)
  local copies, waits for them, and re-layouts: 2.26 us -> 0.97 us
    unnamed x1, local copies, waits for them, and re-layouts: 2.26 us -> 0.97 us
where the time goes in v4:
time: 73.2 us; the launch traced here: 73 us
  Pallas kernels  72.1 us (98%)
  local copies, waits for them, and re-layouts  0.97 us (1%)
    pallas_call x1, Pallas kernels, on_device(): pl.pallas_call(kernel, out_shape=jax.ShapeDtypeStruct(amp.shape, BF), in_...  72.1 us

profile of v4, /device:TPU:1, one launch (start us, length us, event | category | flops | bytes accessed | tf_op | source)
XLA Modules:
  0.0 73.0 jit_solution(4939212918065002729)
XLA Ops:
  0.0 72.1 %cycle.1 = bf16[4,4,2,128,128]{4,3,2,1,0:T(8,128)(2,1)S(1)} custom-call(bf16[4,4,2,128,128]{4,3,2,1,0:T(8,128)(2,1)} %bitcast.5, bf16[28,8,128]{2,1,0:T(8,128)(2,1)} %bitcast.6, f32[32]{0:T(128)} %first_hbm.1, f32[8]{0:T(128)} %second_hbm.1, f32[8,128]{1,0:T(8,128)} %bitcast.7), custom_call_target="tpu_custom_call" | custom-call | tf_op jit(solution)/shard_map/cycle/pallas_call | solution.py:378
  72.1 1.0 %copy.7 = bf16[4,1024,128]{2,1,0:T(8,128)(2,1)} copy(bf16[4,1024,128]{2,1,0:T(8,128)(2,1)S(1)} %bitcast.4) | data formatting | bytes 2097152
